TPU v7x, 32 devices: a whole 2x2x4 slice. The times are simulated.
32 devices in a mesh: sect: 2 (over x), seq: 4 (over y, core), dp: 4 (over z).
Axes of the slice: x: 2, y: 2, z: 4, core: 2. Of those that a mesh axis runs over, the one named last changes fastest.
Arguments:
- query_tiles: bfloat16 [4, 8, 128, 2048], P('dp', None, 'sect', 'seq'), may hold values from -6 to 6
- key_tiles: bfloat16 [4, 8, 128, 2048], P('dp', None, 'sect', 'seq'), may hold values from -6 to 6
- value_tiles: bfloat16 [4, 8, 128, 2048], P('dp', None, 'sect', 'seq'), may hold values from -6 to 6
- text_keys: bfloat16 [8, 256, 2048], P(('sect', 'dp'), 'seq'), may hold values from -6 to 6
- text_values: bfloat16 [8, 256, 2048], P(('sect', 'dp'), 'seq'), may hold values from -6 to 6
- text_lengths: int32 [8], P(('sect', 'dp')), may hold values from 32 to 256, as said below
- tile_place: int32 [4], replicated, may hold values from 0 to 3, each once
Outputs:
- attended: bfloat16 [8, 512, 2048], P(('sect', 'dp'), 'seq')
Inputs may be any that keep to these rules, and one draw needn't show every extreme that they name: `tile_place`: each spatial position is held by exactly one tile slot. `text_lengths`: the live text tokens of a clip are its first rows; some clip fills all 256 slots.
All inputs are finite; a program needn't handle non-finite values.
Results may differ from a plain program's by a relative error of at most 0.0031.
Values may be sent and summed in bfloat16 or wider, within the bound.
A program may use at most 64 MiB of HBM per device.

v0:
```python
import math
import jax
import jax.numpy as jnp
from jax import lax
from jax.sharding import PartitionSpec as P

HD = 128


def attend(queries_flat, keys_video, values_video, keys_text, values_text, length):
    query_rows, head_width = queries_flat.shape
    head_count = head_width // HD
    score_scale = 1.0 / math.sqrt(HD)
    keys_video = keys_video.reshape(-1, head_count, HD)
    values_video = values_video.reshape(-1, head_count, HD)
    keys_text = keys_text.reshape(-1, head_count, HD)
    values_text = values_text.reshape(-1, head_count, HD)
    live_mask = jnp.arange(keys_text.shape[0], dtype=jnp.int32) < length
    block_rows = math.gcd(query_rows, 512)

    def one_block(query_block):
        score_video = (
            jnp.einsum("qhd,khd->hqk", query_block, keys_video, preferred_element_type=jnp.float32)
            * score_scale
        )
        score_text = (
            jnp.einsum("qhd,khd->hqk", query_block, keys_text, preferred_element_type=jnp.float32)
            * score_scale
        )
        score_text = jnp.where(live_mask[None, None, :], score_text, -jnp.inf)
        row_max = jnp.maximum(jnp.max(score_video, axis=-1), jnp.max(score_text, axis=-1))[
            ..., None
        ]
        expo_video = jnp.exp(score_video - row_max)
        expo_text = jnp.exp(score_text - row_max)
        denominators = jnp.sum(expo_video, axis=-1) + jnp.sum(expo_text, axis=-1)
        mixed = jnp.einsum(
            "hqk,khd->qhd",
            expo_video.astype(jnp.bfloat16),
            values_video,
            preferred_element_type=jnp.float32,
        )
        mixed = mixed + jnp.einsum(
            "hqk,khd->qhd",
            expo_text.astype(jnp.bfloat16),
            values_text,
            preferred_element_type=jnp.float32,
        )
        return (mixed / jnp.transpose(denominators)[:, :, None]).astype(jnp.bfloat16)

    blocks = queries_flat.reshape(query_rows // block_rows, block_rows, head_count, HD)
    return lax.map(one_block, blocks).reshape(query_rows, head_width)


def shards(query_tiles, key_tiles, value_tiles, text_keys, text_values, text_lengths, tile_place):
    tile_count = lax.axis_size("dp")
    sect_count = lax.axis_size("sect")
    part_rows = query_tiles.shape[2]
    head_width = query_tiles.shape[3]
    tile_seq = part_rows * sect_count

    def regroup(piece):
        return piece.reshape(1, sect_count, tile_count, part_rows, head_width)

    relayed = (
        lax.all_to_all(
            lax.all_to_all(regroup(query_tiles), "sect", split_axis=1, concat_axis=3, tiled=True),
            "dp",
            split_axis=2,
            concat_axis=0,
            tiled=True,
        ),
        lax.all_to_all(
            lax.all_to_all(regroup(key_tiles), "sect", split_axis=1, concat_axis=3, tiled=True),
            "dp",
            split_axis=2,
            concat_axis=0,
            tiled=True,
        ),
        lax.all_to_all(
            lax.all_to_all(regroup(value_tiles), "sect", split_axis=1, concat_axis=3, tiled=True),
            "dp",
            split_axis=2,
            concat_axis=0,
            tiled=True,
        ),
    )
    spatial_order = jnp.argsort(tile_place)
    seq_count = lax.axis_size("seq")
    tile_rows = tile_seq // seq_count

    def arrange(piece):
        grid = piece.reshape(tile_count, seq_count, tile_rows, head_width)
        placed = jnp.take(grid, spatial_order, axis=0)
        placed = jnp.transpose(placed, (1, 0, 2, 3))
        return placed.reshape(seq_count * tile_count * tile_rows, head_width)

    video_queries = arrange(relayed[0])
    video_keys = arrange(relayed[1])
    video_values = arrange(relayed[2])
    keys_text, values_text = (
        lax.all_to_all(text_keys[0], "seq", split_axis=1, concat_axis=0, tiled=True),
        lax.all_to_all(text_values[0], "seq", split_axis=1, concat_axis=0, tiled=True),
    )
    attended_heads = attend(
        video_queries, video_keys, video_values, keys_text, values_text, text_lengths[0]
    )
    attended = lax.all_to_all(attended_heads, "seq", split_axis=0, concat_axis=1, tiled=True)
    return attended[None]


def solution(mesh):
    in_specs = (
        P("dp", None, "sect", "seq"),
        P("dp", None, "sect", "seq"),
        P("dp", None, "sect", "seq"),
        P(("sect", "dp"), "seq", None),
        P(("sect", "dp"), "seq", None),
        P(("sect", "dp")),
        P(),
    )
    out_specs = P(("sect", "dp"), "seq", None)
    return jax.shard_map(shards, mesh=mesh, in_specs=in_specs, out_specs=out_specs, check_vma=False)
```

profile of v0, /device:TPU:0, one launch (start us, length us, event | category | flops | bytes accessed | tf_op | source)
XLA Modules:
  0.0 116.4 jit_solution(8662692775523040408)
XLA Ops:
  0.0 1.2 %all_to_all.111 = bf16[64,4,512]{2,1,0:T(4,128)(2,1)S(1)} reshape(bf16[1,64,2048]{2,1,0:T(8,128)(2,1)} %param.12) | data formatting | bytes 524288 | tf_op jit(solution)/shard_map/all_to_all | solution.py:102
  1.2 0.7 copy.57
  2.0 4.2 %all-to-all-start.6 = ((bf16[64,4,512]{2,0,1:T(8,128)(2,1)}), bf16[64,4,512]{2,0,1:T(8,128)(2,1)S(1)}, u32[]{:S(2)}, u32[]{:S(2)}) async-start(bf16[64,4,512]{2,0,1:T(8,128)(2,1)} %copy.57), calls=%async_computation.6 | async-start | bytes 524288 | tf_op jit(solution)/shard_map/all_to_all | solution.py:102
  6.2 1.1 all_to_all.114
  7.4 4.8 %all-to-all-done.6 = bf16[64,4,512]{2,0,1:T(8,128)(2,1)S(1)} async-done(((bf16[64,4,512]{2,0,1:T(8,128)(2,1)}), bf16[64,4,512]{2,0,1:T(8,128)(2,1)S(1)}, u32[]{:S(2)}, u32[]{:S(2)}) %all-to-all-start.6) | async-done | bytes 262176 | tf_op jit(solution)/shard_map/all_to_all | solution.py:102
  12.3 8.4 %all_to_all.129 = bf16[64,4,512]{2,0,1:T(8,128)(2,1)S(1)} all-to-all(bf16[64,4,512]{2,0,1:T(8,128)(2,1)S(1)} %copy.62), channel_id=1, replica_groups=mesh['sect'=2,'seq'=4,'dp'=4] {'seq'}, dimensions={1} | all-to-all | bytes 524288 | tf_op jit(solution)/shard_map/all_to_all | solution.py:103
  20.7 10.7 %all_to_all.130 = bf16[1,2,4,64,512]{4,3,2,0,1:T(8,128)(2,1)S(1)} all-to-all(bf16[1,2,4,64,512]{4,3,2,0,1:T(8,128)(2,1)S(1)} %bitcast.72), channel_id=1, replica_groups=mesh['sect'=2,'seq'=4,'dp'=4] {'sect'}, dimensions={1} | all-to-all | bytes 1048576 | tf_op jit(solution)/shard_map/all_to_all | solution.py:67
  31.4 9.1 %all_to_all.131 = bf16[1,2,4,64,512]{4,3,2,0,1:T(8,128)(2,1)S(1)} all-to-all(bf16[1,2,4,64,512]{4,3,2,0,1:T(8,128)(2,1)S(1)} %bitcast.73), channel_id=1, replica_groups=mesh['sect'=2,'seq'=4,'dp'=4] {'sect'}, dimensions={1} | all-to-all | bytes 1048576 | tf_op jit(solution)/shard_map/all_to_all | solution.py:74
  40.5 3.5 %all-to-all-start = ((bf16[1,2,4,64,512]{4,3,2,0,1:T(8,128)(2,1)}), bf16[1,2,4,64,512]{4,3,2,0,1:T(8,128)(2,1)S(1)}, u32[]{:S(2)}, u32[]{:S(2)}) async-start(bf16[1,2,4,64,512]{4,3,2,0,1:T(8,128)(2,1)} %bitcast.1), calls=%async_computation | async-start | bytes 1048576 | tf_op jit(solution)/shard_map/all_to_all | solution.py:81
  44.0 0.8 copy.48
  44.8 5.7 %all-to-all-done = bf16[1,2,4,64,512]{4,3,2,0,1:T(8,128)(2,1)S(1)} async-done(((bf16[1,2,4,64,512]{4,3,2,0,1:T(8,128)(2,1)}), bf16[1,2,4,64,512]{4,3,2,0,1:T(8,128)(2,1)S(1)}, u32[]{:S(2)}, u32[]{:S(2)}) %all-to-all-start) | async-done | bytes 524320 | tf_op jit(solution)/shard_map/all_to_all | solution.py:81
  50.6 5.1 %all-to-all-start.3 = ((bf16[1,1,4,128,512]{4,3,1,0,2:T(8,128)(2,1)}), bf16[1,1,4,128,512]{4,3,1,0,2:T(8,128)(2,1)S(1)}, u32[]{:S(2)}, u32[]{:S(2)}) async-start(bf16[1,1,4,128,512]{4,3,1,0,2:T(8,128)(2,1)} %bitcast.13), calls=%async_computation.3 | async-start | bytes 1048576 | tf_op jit(solution)/shard_map/all_to_all | solution.py:66
  55.7 0.8 copy.52
  56.5 10.1 %all-to-all-done.3 = bf16[1,1,4,128,512]{4,3,1,0,2:T(8,128)(2,1)S(1)} async-done(((bf16[1,1,4,128,512]{4,3,1,0,2:T(8,128)(2,1)}), bf16[1,1,4,128,512]{4,3,1,0,2:T(8,128)(2,1)S(1)}, u32[]{:S(2)}, u32[]{:S(2)}) %all-to-all-start.3) | async-done | bytes 524320 | tf_op jit(solution)/shard_map/all_to_all | solution.py:66
  66.7 3.5 %all-to-all-start.5 = ((bf16[1,1,4,128,512]{4,3,1,0,2:T(8,128)(2,1)}), bf16[1,1,4,128,512]{4,3,1,0,2:T(8,128)(2,1)S(1)}, u32[]{:S(2)}, u32[]{:S(2)}) async-start(bf16[1,1,4,128,512]{4,3,1,0,2:T(8,128)(2,1)} %bitcast.21), calls=%async_computation.5 | async-start | bytes 1048576 | tf_op jit(solution)/shard_map/all_to_all | solution.py:73
  70.2 0.8 copy.44
  71.0 10.7 %all-to-all-done.5 = bf16[1,1,4,128,512]{4,3,1,0,2:T(8,128)(2,1)S(1)} async-done(((bf16[1,1,4,128,512]{4,3,1,0,2:T(8,128)(2,1)}), bf16[1,1,4,128,512]{4,3,1,0,2:T(8,128)(2,1)S(1)}, u32[]{:S(2)}, u32[]{:S(2)}) %all-to-all-start.5) | async-done | bytes 524320 | tf_op jit(solution)/shard_map/all_to_all | solution.py:73
  81.7 3.5 %all-to-all-start.1 = ((bf16[1,1,4,128,512]{4,3,1,0,2:T(8,128)(2,1)}), bf16[1,1,4,128,512]{4,3,1,0,2:T(8,128)(2,1)S(1)}, u32[]{:S(2)}, u32[]{:S(2)}) async-start(bf16[1,1,4,128,512]{4,3,1,0,2:T(8,128)(2,1)} %bitcast.5), calls=%async_computation.1 | async-start | bytes 1048576 | tf_op jit(solution)/shard_map/all_to_all | solution.py:80
  85.9 0.7 sort.17
  86.6 0.8 reshape.75
  87.5 0.6 gather_fusion.1
  88.0 0.6 gather_fusion.2
  88.6 8.7 %all-to-all-done.1 = bf16[1,1,4,128,512]{4,3,1,0,2:T(8,128)(2,1)S(1)} async-done(((bf16[1,1,4,128,512]{4,3,1,0,2:T(8,128)(2,1)}), bf16[1,1,4,128,512]{4,3,1,0,2:T(8,128)(2,1)S(1)}, u32[]{:S(2)}, u32[]{:S(2)}) %all-to-all-start.1) | async-done | bytes 524320 | tf_op jit(solution)/shard_map/all_to_all | solution.py:80
  97.3 0.6 gather_fusion
  98.7 0.7 multiply_reduce_fusion
  99.6 0.5 fusion.6
  100.1 0.5 fusion.7
  100.6 0.7 convolution_bitcast_fusion
  101.3 0.7 fusion
  102.0 0.9 fusion.18
  103.2 12.2 %all_to_all.132 = bf16[4,128,512]{1,2,0:T(8,128)(2,1)S(1)} all-to-all(bf16[4,128,512]{1,2,0:T(8,128)(2,1)S(1)} %copy.66), channel_id=1, replica_groups=mesh['sect'=2,'seq'=4,'dp'=4] {'seq'}, dimensions={0} | all-to-all | bytes 1048576 | tf_op jit(solution)/shard_map/all_to_all | solution.py:108
  115.4 1.0 copy.67
  (26 shorter events, 1.3 us)
Async XLA Ops:
  0.0 20.7 %copy-start = (bf16[1,8,64,512]{3,2,1,0:T(8,128)(2,1)S(1)}, bf16[1,8,64,512]{3,2,1,0:T(8,128)(2,1)}, u32[]{:S(2)}) copy-start(bf16[1,8,64,512]{3,2,1,0:T(8,128)(2,1)} %param.9) | copy-start | bytes 1572868
  0.0 31.4 %copy-start.1 = (bf16[1,8,64,512]{3,2,1,0:T(8,128)(2,1)S(1)}, bf16[1,8,64,512]{3,2,1,0:T(8,128)(2,1)}, u32[]{:S(2)}) copy-start(bf16[1,8,64,512]{3,2,1,0:T(8,128)(2,1)} %param.10) | copy-start | bytes 1572868
  2.0 10.3 %all-to-all-start.6 = ((bf16[64,4,512]{2,0,1:T(8,128)(2,1)}), bf16[64,4,512]{2,0,1:T(8,128)(2,1)S(1)}, u32[]{:S(2)}, u32[]{:S(2)}) async-start(bf16[64,4,512]{2,0,1:T(8,128)(2,1)} %copy.57), calls=%async_computation.6 | async-start | bytes 524288 | tf_op jit(solution)/shard_map/all_to_all | solution.py:102
  40.5 10.1 %all-to-all-start = ((bf16[1,2,4,64,512]{4,3,2,0,1:T(8,128)(2,1)}), bf16[1,2,4,64,512]{4,3,2,0,1:T(8,128)(2,1)S(1)}, u32[]{:S(2)}, u32[]{:S(2)}) async-start(bf16[1,2,4,64,512]{4,3,2,0,1:T(8,128)(2,1)} %bitcast.1), calls=%async_computation | async-start | bytes 1048576 | tf_op jit(solution)/shard_map/all_to_all | solution.py:81
  50.6 16.1 %all-to-all-start.3 = ((bf16[1,1,4,128,512]{4,3,1,0,2:T(8,128)(2,1)}), bf16[1,1,4,128,512]{4,3,1,0,2:T(8,128)(2,1)S(1)}, u32[]{:S(2)}, u32[]{:S(2)}) async-start(bf16[1,1,4,128,512]{4,3,1,0,2:T(8,128)(2,1)} %bitcast.13), calls=%async_computation.3 | async-start | bytes 1048576 | tf_op jit(solution)/shard_map/all_to_all | solution.py:66
  55.7 30.1 %copy-start.3 = (s32[4]{0:T(128)S(1)}, s32[4]{0:T(128)}, u32[]{:S(2)}) copy-start(s32[4]{0:T(128)} %param.15) | copy-start | bytes 52
  66.7 15.0 %all-to-all-start.5 = ((bf16[1,1,4,128,512]{4,3,1,0,2:T(8,128)(2,1)}), bf16[1,1,4,128,512]{4,3,1,0,2:T(8,128)(2,1)S(1)}, u32[]{:S(2)}, u32[]{:S(2)}) async-start(bf16[1,1,4,128,512]{4,3,1,0,2:T(8,128)(2,1)} %bitcast.21), calls=%async_computation.5 | async-start | bytes 1048576 | tf_op jit(solution)/shard_map/all_to_all | solution.py:73
  81.7 15.6 %all-to-all-start.1 = ((bf16[1,1,4,128,512]{4,3,1,0,2:T(8,128)(2,1)}), bf16[1,1,4,128,512]{4,3,1,0,2:T(8,128)(2,1)S(1)}, u32[]{:S(2)}, u32[]{:S(2)}) async-start(bf16[1,1,4,128,512]{4,3,1,0,2:T(8,128)(2,1)} %bitcast.5), calls=%async_computation.1 | async-start | bytes 1048576 | tf_op jit(solution)/shard_map/all_to_all | solution.py:80
  98.7 1.0 copy-start.2
where the time goes:
time: 117 us; the launch traced here: 116 us
  blocking collectives  40.4 us (35%)
  waiting for transfers between devices  40.1 us (34%)
  starting transfers between devices  19.8 us (17%)
  local copies, waits for them, and re-layouts  10.2 us (9%)
  matrix products  2.8 us (2%)
  other arithmetic  2.19 us (2%)
    all_to_all x1, blocking collectives, shards(): lax.all_to_all(attended_heads, 'seq', split_axis=0, concat_axis=1, tiled=...  12.2 us
    all_to_all x1, blocking collectives, shards(): lax.all_to_all(regroup(query_tiles), 'sect', split_axis=1, concat_axis=3,...  10.7 us
    all_to_all x1, waiting for transfers between devices, shards(): lax.all_to_all(lax.all_to_all(regroup(key_tiles), 'sect', split_axis=1, c...  10.7 us
    all_to_all x1, waiting for transfers between devices, shards(): lax.all_to_all(lax.all_to_all(regroup(query_tiles), 'sect', split_axis=1,...  10.1 us
    all_to_all x1, blocking collectives, shards(): lax.all_to_all(regroup(key_tiles), 'sect', split_axis=1, concat_axis=3, t...  9.08 us
    all_to_all x1, waiting for transfers between devices, shards(): lax.all_to_all(lax.all_to_all(regroup(value_tiles), 'sect', split_axis=1,...  8.71 us
    all_to_all x1, blocking collectives, shards(): lax.all_to_all(text_values[0], 'seq', split_axis=1, concat_axis=0, tiled=...  8.41 us
    all_to_all x1, waiting for transfers between devices, shards(): lax.all_to_all(regroup(value_tiles), 'sect', split_axis=1, concat_axis=3,...  5.72 us
  transfers between devices with their start and end apart: 5, of which 5 were waited for; matrix products, arithmetic and copies ran while one was open for 5% of the time, Pallas kernels for 0%

commit v1 on v0

--- a/solution.py
+++ b/solution.py
@@ -63,12 +63,22 @@
         return piece.reshape(1, sect_count, tile_count, part_rows, head_width)
 
     relayed = (
-        lax.all_to_all(
-            lax.all_to_all(regroup(query_tiles), "sect", split_axis=1, concat_axis=3, tiled=True),
-            "dp",
-            split_axis=2,
-            concat_axis=0,
-            tiled=True,
+        jnp.concatenate(
+            lax.all_to_all(
+                jnp.stack(
+                    jnp.split(
+                        lax.all_to_all(
+                            regroup(query_tiles), "sect", split_axis=1, concat_axis=3, tiled=True
+                        ),
+                        lax.axis_size("dp"),
+                        axis=2,
+                    )
+                ),
+                "dp",
+                0,
+                0,
+            ),
+            axis=0,
         ),
         lax.all_to_all(
             lax.all_to_all(regroup(key_tiles), "sect", split_axis=1, concat_axis=3, tiled=True),

time: 117 us -> 118 us (level)
  blocking collectives: 40.4 us -> 31.4 us
  waiting for transfers between devices: 40.1 us -> 46.7 us
  starting transfers between devices: 19.8 us -> 23.3 us
    all_to_all x1 -> x0, blocking collectives: 9.08 us -> none  [shards(): lax.all_to_all(regroup(key_tiles), 'sect', split_axis=1, concat_axis=3, t...]
    all_to_all x1 -> x2, waiting for transfers between devices: 10.1 us -> 16.8 us  [the longest x1 10.1 us: shards(): lax.all_to_all(jnp.stack(jnp.split(lax.all_to_all(regroup(query_tiles), '...]
    all_to_all x1 -> x2, starting transfers between devices: 5.14 us -> 8.63 us  [the longest x1 5.14 us: shards(): lax.all_to_all(jnp.stack(jnp.split(lax.all_to_all(regroup(query_tiles), '...]
  transfers between devices with their start and end apart: 5 -> 6, of which waited for: 5 -> 6; matrix products, arithmetic and copies ran while one was open for 5% -> 5% of each run, Pallas kernels for 0% -> 0%
where the time goes in v1:
time: 118 us; the launch traced here: 117 us
  waiting for transfers between devices  46.7 us (40%)
  blocking collectives  31.4 us (27%)
  starting transfers between devices  23.3 us (20%)
  local copies, waits for them, and re-layouts  9.37 us (8%)
  other arithmetic  3.06 us (3%)
  matrix products  2.79 us (2%)
    all_to_all x1, blocking collectives, shards(): lax.all_to_all(attended_heads, 'seq', split_axis=0, concat_axis=1, tiled=...  12.2 us
    all_to_all x1, blocking collectives, shards(): lax.all_to_all(regroup(query_tiles), 'sect', split_axis=1, concat_axis=3,...  10.7 us
    all_to_all x1, waiting for transfers between devices, shards(): lax.all_to_all(lax.all_to_all(regroup(key_tiles), 'sect', split_axis=1, c...  10.7 us
    all_to_all x1, waiting for transfers between devices, shards(): lax.all_to_all(jnp.stack(jnp.split(lax.all_to_all(regroup(query_tiles), '...  10.1 us
    all_to_all x1, waiting for transfers between devices, shards(): lax.all_to_all(lax.all_to_all(regroup(value_tiles), 'sect', split_axis=1,...  8.71 us
    all_to_all x1, blocking collectives, shards(): lax.all_to_all(text_values[0], 'seq', split_axis=1, concat_axis=0, tiled=...  8.41 us
    all_to_all x1, waiting for transfers between devices, shards(): lax.all_to_all(regroup(key_tiles), 'sect', split_axis=1, concat_axis=3, t...  6.63 us
    all_to_all x1, waiting for transfers between devices, shards(): lax.all_to_all(regroup(value_tiles), 'sect', split_axis=1, concat_axis=3,...  5.66 us
  transfers between devices with their start and end apart: 6, of which 6 were waited for; matrix products, arithmetic and copies ran while one was open for 5% of the time, Pallas kernels for 0%

profile of v1, /device:TPU:0, one launch (start us, length us, event | category | flops | bytes accessed | tf_op | source)
XLA Modules:
  0.0 117.4 jit_solution(11450852220471394950)
XLA Ops:
  0.0 1.2 %all_to_all.107 = bf16[64,4,512]{2,1,0:T(4,128)(2,1)S(1)} reshape(bf16[1,64,2048]{2,1,0:T(8,128)(2,1)} %param.12) | data formatting | bytes 524288 | tf_op jit(solution)/shard_map/all_to_all | solution.py:112
  1.2 0.7 copy.56
  1.9 4.2 %all-to-all-start.6 = ((bf16[64,4,512]{2,0,1:T(8,128)(2,1)}), bf16[64,4,512]{2,0,1:T(8,128)(2,1)S(1)}, u32[]{:S(2)}, u32[]{:S(2)}) async-start(bf16[64,4,512]{2,0,1:T(8,128)(2,1)} %copy.56), calls=%async_computation.6 | async-start | bytes 524288 | tf_op jit(solution)/shard_map/all_to_all | solution.py:112
  6.2 1.1 all_to_all.110
  7.4 4.8 %all-to-all-done.6 = bf16[64,4,512]{2,0,1:T(8,128)(2,1)S(1)} async-done(((bf16[64,4,512]{2,0,1:T(8,128)(2,1)}), bf16[64,4,512]{2,0,1:T(8,128)(2,1)S(1)}, u32[]{:S(2)}, u32[]{:S(2)}) %all-to-all-start.6) | async-done | bytes 262176 | tf_op jit(solution)/shard_map/all_to_all | solution.py:112
  12.2 8.4 %all_to_all.125 = bf16[64,4,512]{2,0,1:T(8,128)(2,1)S(1)} all-to-all(bf16[64,4,512]{2,0,1:T(8,128)(2,1)S(1)} %copy.61), channel_id=1, replica_groups=mesh['sect'=2,'seq'=4,'dp'=4] {'seq'}, dimensions={1} | all-to-all | bytes 524288 | tf_op jit(solution)/shard_map/all_to_all | solution.py:113
  20.6 10.7 %all_to_all.126 = bf16[1,2,4,64,512]{4,3,2,0,1:T(8,128)(2,1)S(1)} all-to-all(bf16[1,2,4,64,512]{4,3,2,0,1:T(8,128)(2,1)S(1)} %bitcast.79), channel_id=1, replica_groups=mesh['sect'=2,'seq'=4,'dp'=4] {'sect'}, dimensions={1} | all-to-all | bytes 1048576 | tf_op jit(solution)/shard_map/all_to_all | solution.py:70
  31.4 3.5 %all-to-all-start.4 = ((bf16[1,2,4,64,512]{4,3,2,0,1:T(8,128)(2,1)}), bf16[1,2,4,64,512]{4,3,2,0,1:T(8,128)(2,1)S(1)}, u32[]{:S(2)}, u32[]{:S(2)}) async-start(bf16[1,2,4,64,512]{4,3,2,0,1:T(8,128)(2,1)} %bitcast.22), calls=%async_computation.4 | async-start | bytes 1048576 | tf_op jit(solution)/shard_map/all_to_all | solution.py:84
  34.9 6.6 %all-to-all-done.4 = bf16[1,2,4,64,512]{4,3,2,0,1:T(8,128)(2,1)S(1)} async-done(((bf16[1,2,4,64,512]{4,3,2,0,1:T(8,128)(2,1)}), bf16[1,2,4,64,512]{4,3,2,0,1:T(8,128)(2,1)S(1)}, u32[]{:S(2)}, u32[]{:S(2)}) %all-to-all-start.4) | async-done | bytes 524320 | tf_op jit(solution)/shard_map/all_to_all | solution.py:84
  41.6 3.5 %all-to-all-start = ((bf16[1,2,4,64,512]{4,3,2,0,1:T(8,128)(2,1)}), bf16[1,2,4,64,512]{4,3,2,0,1:T(8,128)(2,1)S(1)}, u32[]{:S(2)}, u32[]{:S(2)}) async-start(bf16[1,2,4,64,512]{4,3,2,0,1:T(8,128)(2,1)} %bitcast.1), calls=%async_computation | async-start | bytes 1048576 | tf_op jit(solution)/shard_map/all_to_all | solution.py:91
  45.1 0.9 pad_maximum_fusion
  46.0 5.7 %all-to-all-done = bf16[1,2,4,64,512]{4,3,2,0,1:T(8,128)(2,1)S(1)} async-done(((bf16[1,2,4,64,512]{4,3,2,0,1:T(8,128)(2,1)}), bf16[1,2,4,64,512]{4,3,2,0,1:T(8,128)(2,1)S(1)}, u32[]{:S(2)}, u32[]{:S(2)}) %all-to-all-start) | async-done | bytes 524320 | tf_op jit(solution)/shard_map/all_to_all | solution.py:91
  51.6 5.1 %all-to-all-start.3 = ((bf16[4,1,1,1,128,512]{5,4,3,2,1,0:T(8,128)(2,1)}), bf16[4,1,1,1,128,512]{5,4,3,2,1,0:T(8,128)(2,1)S(1)}, u32[]{:S(2)}, u32[]{:S(2)}) async-start(bf16[4,1,1,1,128,512]{5,4,3,2,1,0:T(8,128)(2,1)} %pad_maximum_fusion), calls=%async_computation.3 | async-start | bytes 1048576 | tf_op jit(solution)/shard_map/all_to_all | solution.py:67
  56.8 0.8 copy.51
  57.6 10.1 %all-to-all-done.3 = bf16[4,1,1,1,128,512]{5,4,3,2,1,0:T(8,128)(2,1)S(1)} async-done(((bf16[4,1,1,1,128,512]{5,4,3,2,1,0:T(8,128)(2,1)}), bf16[4,1,1,1,128,512]{5,4,3,2,1,0:T(8,128)(2,1)S(1)}, u32[]{:S(2)}, u32[]{:S(2)}) %all-to-all-start.3) | async-done | bytes 524320 | tf_op jit(solution)/shard_map/all_to_all | solution.py:67
  67.7 3.5 %all-to-all-start.5 = ((bf16[1,1,4,128,512]{4,3,1,0,2:T(8,128)(2,1)}), bf16[1,1,4,128,512]{4,3,1,0,2:T(8,128)(2,1)S(1)}, u32[]{:S(2)}, u32[]{:S(2)}) async-start(bf16[1,1,4,128,512]{4,3,1,0,2:T(8,128)(2,1)} %bitcast.26), calls=%async_computation.5 | async-start | bytes 1048576 | tf_op jit(solution)/shard_map/all_to_all | solution.py:83
  71.2 0.8 copy.44
  72.1 10.7 %all-to-all-done.5 = bf16[1,1,4,128,512]{4,3,1,0,2:T(8,128)(2,1)S(1)} async-done(((bf16[1,1,4,128,512]{4,3,1,0,2:T(8,128)(2,1)}), bf16[1,1,4,128,512]{4,3,1,0,2:T(8,128)(2,1)S(1)}, u32[]{:S(2)}, u32[]{:S(2)}) %all-to-all-start.5) | async-done | bytes 524320 | tf_op jit(solution)/shard_map/all_to_all | solution.py:83
  82.8 3.5 %all-to-all-start.1 = ((bf16[1,1,4,128,512]{4,3,1,0,2:T(8,128)(2,1)}), bf16[1,1,4,128,512]{4,3,1,0,2:T(8,128)(2,1)S(1)}, u32[]{:S(2)}, u32[]{:S(2)}) async-start(bf16[1,1,4,128,512]{4,3,1,0,2:T(8,128)(2,1)} %bitcast.5), calls=%async_computation.1 | async-start | bytes 1048576 | tf_op jit(solution)/shard_map/all_to_all | solution.py:90
  86.9 0.7 sort.17
  87.7 0.8 reshape.67
  88.5 0.6 gather_fusion.1
  89.1 0.6 gather_fusion.2
  89.7 8.7 %all-to-all-done.1 = bf16[1,1,4,128,512]{4,3,1,0,2:T(8,128)(2,1)S(1)} async-done(((bf16[1,1,4,128,512]{4,3,1,0,2:T(8,128)(2,1)}), bf16[1,1,4,128,512]{4,3,1,0,2:T(8,128)(2,1)S(1)}, u32[]{:S(2)}, u32[]{:S(2)}) %all-to-all-start.1) | async-done | bytes 524320 | tf_op jit(solution)/shard_map/all_to_all | solution.py:90
  98.4 0.6 gather_fusion
  99.7 0.7 multiply_reduce_fusion
  101.2 0.5 fusion.7
  101.7 0.7 convolution_bitcast_fusion
  102.3 0.7 fusion
  103.1 0.9 fusion.18
  104.2 12.2 %all_to_all.127 = bf16[4,128,512]{1,2,0:T(8,128)(2,1)S(1)} all-to-all(bf16[4,128,512]{1,2,0:T(8,128)(2,1)S(1)} %copy.65), channel_id=1, replica_groups=mesh['sect'=2,'seq'=4,'dp'=4] {'seq'}, dimensions={0} | all-to-all | bytes 1048576 | tf_op jit(solution)/shard_map/all_to_all | solution.py:118
  116.4 1.0 copy.66
  (27 shorter events, 1.8 us)
Async XLA Ops:
  0.0 20.6 %copy-start = (bf16[1,8,64,512]{3,2,1,0:T(8,128)(2,1)S(1)}, bf16[1,8,64,512]{3,2,1,0:T(8,128)(2,1)}, u32[]{:S(2)}) copy-start(bf16[1,8,64,512]{3,2,1,0:T(8,128)(2,1)} %param.9) | copy-start | bytes 1572868
  1.9 10.3 %all-to-all-start.6 = ((bf16[64,4,512]{2,0,1:T(8,128)(2,1)}), bf16[64,4,512]{2,0,1:T(8,128)(2,1)S(1)}, u32[]{:S(2)}, u32[]{:S(2)}) async-start(bf16[64,4,512]{2,0,1:T(8,128)(2,1)} %copy.56), calls=%async_computation.6 | async-start | bytes 524288 | tf_op jit(solution)/shard_map/all_to_all | solution.py:112
  31.4 10.2 %all-to-all-start.4 = ((bf16[1,2,4,64,512]{4,3,2,0,1:T(8,128)(2,1)}), bf16[1,2,4,64,512]{4,3,2,0,1:T(8,128)(2,1)S(1)}, u32[]{:S(2)}, u32[]{:S(2)}) async-start(bf16[1,2,4,64,512]{4,3,2,0,1:T(8,128)(2,1)} %bitcast.22), calls=%async_computation.4 | async-start | bytes 1048576 | tf_op jit(solution)/shard_map/all_to_all | solution.py:84
  41.6 10.1 %all-to-all-start = ((bf16[1,2,4,64,512]{4,3,2,0,1:T(8,128)(2,1)}), bf16[1,2,4,64,512]{4,3,2,0,1:T(8,128)(2,1)S(1)}, u32[]{:S(2)}, u32[]{:S(2)}) async-start(bf16[1,2,4,64,512]{4,3,2,0,1:T(8,128)(2,1)} %bitcast.1), calls=%async_computation | async-start | bytes 1048576 | tf_op jit(solution)/shard_map/all_to_all | solution.py:91
  51.6 16.1 %all-to-all-start.3 = ((bf16[4,1,1,1,128,512]{5,4,3,2,1,0:T(8,128)(2,1)}), bf16[4,1,1,1,128,512]{5,4,3,2,1,0:T(8,128)(2,1)S(1)}, u32[]{:S(2)}, u32[]{:S(2)}) async-start(bf16[4,1,1,1,128,512]{5,4,3,2,1,0:T(8,128)(2,1)} %pad_maximum_fusion), calls=%async_computation.3 | async-start | bytes 1048576 | tf_op jit(solution)/shard_map/all_to_all | solution.py:67
  56.8 30.1 %copy-start.2 = (s32[4]{0:T(128)S(1)}, s32[4]{0:T(128)}, u32[]{:S(2)}) copy-start(s32[4]{0:T(128)} %param.15) | copy-start | bytes 52
  67.7 15.0 %all-to-all-start.5 = ((bf16[1,1,4,128,512]{4,3,1,0,2:T(8,128)(2,1)}), bf16[1,1,4,128,512]{4,3,1,0,2:T(8,128)(2,1)S(1)}, u32[]{:S(2)}, u32[]{:S(2)}) async-start(bf16[1,1,4,128,512]{4,3,1,0,2:T(8,128)(2,1)} %bitcast.26), calls=%async_computation.5 | async-start | bytes 1048576 | tf_op jit(solution)/shard_map/all_to_all | solution.py:83
  82.8 15.6 %all-to-all-start.1 = ((bf16[1,1,4,128,512]{4,3,1,0,2:T(8,128)(2,1)}), bf16[1,1,4,128,512]{4,3,1,0,2:T(8,128)(2,1)S(1)}, u32[]{:S(2)}, u32[]{:S(2)}) async-start(bf16[1,1,4,128,512]{4,3,1,0,2:T(8,128)(2,1)} %bitcast.5), calls=%async_computation.1 | async-start | bytes 1048576 | tf_op jit(solution)/shard_map/all_to_all | solution.py:90
  99.7 1.0 copy-start.1
